TPU v7x, 32 devices: a whole 2x2x4 slice. The times are simulated.
32 devices in a mesh: row: 4 (over z), col: 4 (over x, core), depth: 2 (over y).
Axes of the slice: x: 2, y: 2, z: 4, core: 2. Of those that a mesh axis runs over, the one named last changes fastest.
Arguments:
- left_block: bfloat16 [4, 8192, 512], P(None, ('row', 'depth'), 'col'), may hold values from -6 to 6
- right_block: bfloat16 [512, 2, 16384], P(('row', 'depth'), None, 'col'), may hold values from -0.125 to 0.125
- slice_ids: int32 [4], replicated, may hold values from 0 to 1, as said below
- mode_order: int32 [9], replicated, may hold values from 0 to 8, each once
Outputs:
- contracted: float32 [8192, 16384], P(('row', 'depth'), 'col')
Inputs may be any that keep to these rules, and one draw needn't show every extreme that they name: mode_order holds every number of 0 to 8 once. `slice_ids`: each value of the sliced bond is taken by exactly 2 slices.
All inputs are finite; a program needn't handle non-finite values.
Results may differ from a plain program's by a relative error of at most 0.0003.
Values may be sent and summed in bfloat16 or wider, within the bound.
No kernel may reach another device: no remote copies, remote signals or barrier semaphores. Data moves between devices by JAX's collectives and lax.ppermute only.
A program may use at most 128 MiB of HBM per device.

v0:
```python
import jax
import jax.numpy as jnp
from jax import lax
from jax.sharding import PartitionSpec as P


def stored_order(mode_order, columns):
    logical = jnp.arange(columns, dtype=jnp.int32)
    stored = jnp.zeros((columns,), jnp.int32)
    for bit_place in range(mode_order.shape[0]):
        stored = stored + logical // 2**bit_place % 2 * jnp.left_shift(
            jnp.int32(1), mode_order[bit_place]
        )
    return stored


def per_device(left_block, right_block, slice_ids, mode_order):
    values = right_block.shape[1]
    picks = (slice_ids[:, None] == jnp.arange(values, dtype=jnp.int32)[None, :]).astype(jnp.float32)
    folded = jnp.zeros((values,) + left_block.shape[1:], jnp.float32)
    for number in range(left_block.shape[0]):
        folded = (
            folded + picks[number][:, None, None] * left_block[number].astype(jnp.float32)[None]
        )
    whole_left = lax.all_gather(folded, "col", axis=2, tiled=True)
    permuted = jnp.take(whole_left, stored_order(mode_order, whole_left.shape[2]), axis=2)
    return jnp.einsum(
        "crk,kcn->rn",
        permuted,
        lax.all_gather(right_block, ("row", "depth"), axis=0, tiled=True).astype(jnp.float32),
        preferred_element_type=jnp.float32,
        precision=lax.Precision.HIGHEST,
    )


def solution(mesh):
    in_specs = (P(None, ("row", "depth"), "col"), P(("row", "depth"), None, "col"), P(), P())
    out_specs = P(("row", "depth"), "col")
    return jax.shard_map(
        per_device, mesh=mesh, in_specs=in_specs, out_specs=out_specs, check_vma=False
    )
```

profile of v0, /device:TPU:0, one launch (start us, length us, event | category | flops | bytes accessed | tf_op | source)
XLA Modules:
  0.0 218.0 jit_solution(17528352882170684913)
XLA Ops:
  6.5 0.0 all-gather.3.cloned.1.call-start
  6.5 0.7 fusion.70
  7.3 1.3 bitcast_convert_fusion.3
  8.6 0.2 copy.12
  8.8 0.2 copy.13
  9.0 0.2 copy.15
  9.2 0.0 copy-start
  9.2 0.2 copy.14
  9.4 1.9 multiply_add_fusion
  11.3 0.0 all-gather.3.cloned.1.call-update
  11.4 0.0 all-gather.5.cloned.1.call-start
  11.4 2.8 %copy.16 = bf16[64,2,4096]{2,0,1:T(8,128)(2,1)} copy(bf16[64,2,4096]{2,1,0:T(2,128)(2,1)} %param.5) | data formatting | bytes 2097152 | tf_op args[1]
  14.3 0.0 all-gather.5.cloned.1.call-update
  14.3 0.0 copy-done
  14.3 0.7 fusion.71
  20.7 28.0 %all-gather.3.cloned.1.call-done = f32[2,1024,512]{1,0,2:T(2,128)} async-done(((f32[2,1024,128]{1,0,2:T(2,128)}), f32[2,1024,512]{1,0,2:T(2,128)}) %all-gather.3.cloned.1.call-update) | async-done | bytes 4194320 | tf_op jit(solution)/shard_map/all_gather | solution.py:25
  48.7 21.9 %gather_fusion = f32[512,2,1024]{2,1,0:T(2,128)} fusion(f32[2,1024,512]{1,0,2:T(2,128)} %all-gather.3.cloned.1.call-done, s32[1024]{0:T(1024)S(1)} %pad_clamp_fusion), kind=kCustom, calls=%fused_computation | custom fusion | bytes 8390656 | tf_op jit(solution)/shard_map/jit(_take)/gather | solution.py:26
  70.6 6.0 %select_bitcast_fusion = f32[2,1024,512]{1,0,2:T(2,128)} fusion(f32[512,2,1024]{2,1,0:T(2,128)} %gather_fusion, pred[512]{0:T(512)(128)(4,1)S(1)} %compare_and_fusion), kind=kLoop, calls=%fused_computation.3 | loop fusion | flops 1048576 | bytes 8389120 | tf_op jit(solution)/shard_map/jit(_take)/select_n | solution.py:26
  76.6 98.8 %all-gather.5.cloned.1.call-done = bf16[512,2,4096]{2,0,1:T(8,128)(2,1)} async-done(((bf16[64,2,4096]{2,0,1:T(8,128)(2,1)}), bf16[512,2,4096]{2,0,1:T(8,128)(2,1)}) %all-gather.5.cloned.1.call-update) | async-done | bytes 8388624 | tf_op jit(solution)/shard_map/all_gather | solution.py:30
  175.4 35.8 %convolution_bitcast_fusion = f32[1024,4096]{1,0:T(8,128)} fusion(bf16[512,2,4096]{2,0,1:T(8,128)(2,1)} %all-gather.5.cloned.1.call-done, f32[2,1024,512]{1,0,2:T(2,128)} %select_bitcast_fusion), kind=kOutput, calls=%fused_computation.1 | convolution fusion | flops 51539607552 | bytes 29360128 | tf_op jit(solution)/shard_map/crk,kcn->rn/dot_general | solution.py:27
  (4 shorter events, 0.1 us)
Async XLA Ops:
  6.5 42.2 %all-gather.3.cloned.1.call-start = ((), (), s32[]{:S(2)}) async-start(), calls=%async_computation | async-start | bytes 5242880 | tf_op jit(solution)/shard_map/all_gather | solution.py:25
  9.2 5.1 %copy-start = (s32[9]{0:T(128)S(1)}, s32[9]{0:T(128)}, u32[]{:S(2)}) copy-start(s32[9]{0:T(128)} %param.7) | copy-start | bytes 112
  11.4 164.0 %all-gather.5.cloned.1.call-start = ((), (), s32[]{:S(2)}) async-start(), calls=%async_computation.1 | async-start | bytes 9437184 | tf_op jit(solution)/shard_map/all_gather | solution.py:30
Sparse Core Ops, SparseCore 0:
  11.5 37.1 all-gather.2
  50.9 124.4 all-gather.4
where the time goes:
time: 218 us
  waiting for transfers between devices  127 us (58%)
  matrix products  35.8 us (16%)
  local copies, waits for them, and re-layouts  26.2 us (12%)
  between operations  19.1 us (9%)
  other arithmetic  10 us (5%)
    all_gather x1, waiting for transfers between devices, per_device(): lax.all_gather(right_block, ('row', 'depth'), axis=0, tiled=True)  98.8 us
    dot_general x1, matrix products, per_device(): jnp.einsum('crk,kcn->rn', permuted, lax.all_gather(right_block, ('row', '...  35.8 us
    all_gather x1, waiting for transfers between devices, per_device(): whole_left = lax.all_gather(folded, 'col', axis=2, tiled=True)  28 us
    gather x1, local copies, waits for them, and re-layouts, per_device(): jnp.take(whole_left, stored_order(mode_order, whole_left.shape[2]), axis=2)  21.9 us
    select_n x2, other arithmetic, per_device(): jnp.take(whole_left, stored_order(mode_order, whole_left.shape[2]), axis=2)  6.06 us
  transfers between devices with their start and end apart: 2, of which 2 were waited for; matrix products, arithmetic and copies ran while one was open for 14% of the time, Pallas kernels for 0%

commit v1 on v0

--- a/solution.py
+++ b/solution.py
@@ -22,7 +22,13 @@
         folded = (
             folded + picks[number][:, None, None] * left_block[number].astype(jnp.float32)[None]
         )
-    whole_left = lax.all_gather(folded, "col", axis=2, tiled=True)
+    size = lax.axis_size("col")
+    block, blocks = (folded, [folded])
+    for _ in range(size - 1):
+        block = lax.ppermute(block, "col", [(i, (i + 1) % size) for i in range(size)])
+        blocks.insert(0, block)
+    flat = jnp.concatenate(blocks, axis=2)
+    whole_left = jnp.roll(flat, (lax.axis_index("col") + 1) * folded.shape[2], axis=2)
     permuted = jnp.take(whole_left, stored_order(mode_order, whole_left.shape[2]), axis=2)
     return jnp.einsum(
         "crk,kcn->rn",

time: 218 us -> 180 us (0.83)
  waiting for transfers between devices: 127 us -> 77.4 us
  local copies, waits for them, and re-layouts: 26.2 us -> 35.4 us
    all_gather x1, waiting for transfers between devices: 98.8 us -> 40.5 us  [per_device(): lax.all_gather(right_block, ('row', 'depth'), axis=0, tiled=True)]
    ppermute x0 -> x3, waiting for transfers between devices: none -> 36.9 us  [per_device(): lax.ppermute(block, 'col', [(i, (i + 1) % size) for i in range(size)])]
    all_gather x1 -> x0, waiting for transfers between devices: 28 us -> none  [per_device(): whole_left = lax.all_gather(folded, 'col', axis=2, tiled=True)]
    unnamed x3 -> x11, local copies, waits for them, and re-layouts: 2.85 us -> 8.54 us
    dynamic_slice x0 -> x1, local copies, waits for them, and re-layouts: none -> 3.46 us  [per_device(): jnp.roll(flat, (lax.axis_index('col') + 1) * folded.shape[2], axis=2)]
  transfers between devices with their start and end apart: 2 -> 4, of which waited for: 2 -> 4; matrix products, arithmetic and copies ran while one was open for 14% -> 24% of each run, Pallas kernels for 0% -> 0%
where the time goes in v1:
time: 180 us; the launch traced here: 179 us
  waiting for transfers between devices  77.4 us (43%)
  matrix products  35.8 us (20%)
  local copies, waits for them, and re-layouts  35.4 us (20%)
  between operations  19.1 us (11%)
  other arithmetic  11.2 us (6%)
    all_gather x1, waiting for transfers between devices, per_device(): lax.all_gather(right_block, ('row', 'depth'), axis=0, tiled=True)  40.5 us
    ppermute x3, waiting for transfers between devices, per_device(): lax.ppermute(block, 'col', [(i, (i + 1) % size) for i in range(size)])  36.9 us
    dot_general x1, matrix products, per_device(): jnp.einsum('crk,kcn->rn', permuted, lax.all_gather(right_block, ('row', '...  35.8 us
    gather x1, local copies, waits for them, and re-layouts, per_device(): jnp.take(whole_left, stored_order(mode_order, whole_left.shape[2]), axis=2)  21.9 us
    unnamed x11, local copies, waits for them, and re-layouts  8.54 us
    select_n x2, other arithmetic, per_device(): jnp.take(whole_left, stored_order(mode_order, whole_left.shape[2]), axis=2)  6.03 us
  transfers between devices with their start and end apart: 4, of which 4 were waited for; matrix products, arithmetic and copies ran while one was open for 24% of the time, Pallas kernels for 0%

profile of v1, /device:TPU:0, one launch (start us, length us, event | category | flops | bytes accessed | tf_op | source)
XLA Modules:
  0.0 179.4 jit_solution(11012731396946883448)
XLA Ops:
  6.5 2.9 %copy.10 = bf16[64,2,4096]{2,0,1:T(8,128)(2,1)} copy(bf16[64,2,4096]{2,1,0:T(2,128)(2,1)} %param.5) | data formatting | bytes 2097152 | tf_op args[1]
  9.4 1.3 bitcast_convert_fusion.3
  10.8 0.2 copy.6
  11.0 0.2 copy.7
  11.2 0.2 copy.8
  11.4 0.2 copy.9
  11.7 1.1 multiply_add_fusion
  12.8 0.5 collective-permute-start
  13.3 14.4 %collective-permute-done = f32[2,1024,128]{1,0,2:T(2,128)S(1)} collective-permute-done((f32[2,1024,128]{1,0,2:T(2,128)S(1)}, f32[2,1024,128]{1,0,2:T(2,128)S(1)}, u32[]{:S(2)}, u32[]{:S(2)}) %collective-permute-start) | collective-permute-done | bytes 1048608 | tf_op jit(solution)/shard_map/ppermute | solution.py:28
  27.7 14.3 %collective-permute-done.1 = f32[2,1024,128]{1,0,2:T(2,128)} collective-permute-done((f32[2,1024,128]{1,0,2:T(2,128)S(1)}, f32[2,1024,128]{1,0,2:T(2,128)}, u32[]{:S(2)}, u32[]{:S(2)}) %collective-permute-start.1) | collective-permute-done | bytes 1048608 | tf_op jit(solution)/shard_map/ppermute | solution.py:28
  42.1 0.7 fusion.71
  48.4 8.2 %collective-permute-done.2 = f32[2,1024,128]{1,0,2:T(2,128)} collective-permute-done((f32[2,1024,128]{1,0,2:T(2,128)}, f32[2,1024,128]{1,0,2:T(2,128)}, u32[]{:S(2)}, u32[]{:S(2)}) %collective-permute-start.2) | collective-permute-done | bytes 1048608 | tf_op jit(solution)/shard_map/ppermute | solution.py:28
  56.6 1.3 constant_dynamic-update-slice_fusion.7
  57.9 1.4 constant_dynamic-update-slice_fusion.6
  59.3 0.1 constant_dynamic-update-slice_fusion.5
  59.4 1.4 constant_dynamic-update-slice_fusion.4
  60.8 1.4 constant_dynamic-update-slice_fusion.3
  62.2 1.4 constant_dynamic-update-slice_fusion.2
  63.7 1.2 constant_dynamic-update-slice_fusion
  64.9 3.5 %constant_dynamic-slice_fusion = f32[2,1024,512]{1,0,2:T(2,128)} fusion(f32[2,1024,1024]{1,0,2:T(2,128)S(1)} %constant_dynamic-update-slice_fusion, s32[]{:T(128)S(6)} %select_n.306), kind=kLoop, calls=%fused_computation.195 | loop fusion | bytes 8388612 | tf_op jit(solution)/shard_map/jit(_roll_dynamic)/dynamic_slice | solution.py:31
  68.4 21.9 %gather_fusion = f32[512,2,1024]{2,1,0:T(2,128)} fusion(f32[2,1024,512]{1,0,2:T(2,128)} %constant_dynamic-slice_fusion, s32[1024]{0:T(1024)S(1)} %pad_clamp_fusion), kind=kCustom, calls=%fused_computation | custom fusion | bytes 8390656 | tf_op jit(solution)/shard_map/jit(_take)/gather | solution.py:32
  90.3 6.0 %select_bitcast_fusion = f32[2,1024,512]{1,0,2:T(2,128)} fusion(f32[512,2,1024]{2,1,0:T(2,128)} %gather_fusion, pred[512]{0:T(512)(128)(4,1)S(1)} %compare_and_fusion), kind=kLoop, calls=%fused_computation.3 | loop fusion | flops 1048576 | bytes 8389120 | tf_op jit(solution)/shard_map/jit(_take)/select_n | solution.py:32
  96.3 40.5 %all-gather.2.cloned.1.call-done = bf16[512,2,4096]{2,0,1:T(8,128)(2,1)} async-done(((bf16[64,2,4096]{2,0,1:T(8,128)(2,1)}), bf16[512,2,4096]{2,0,1:T(8,128)(2,1)}) %all-gather.2.cloned.1.call-update) | async-done | bytes 8388624 | tf_op jit(solution)/shard_map/all_gather | solution.py:36
  136.8 35.8 %convolution_bitcast_fusion = f32[1024,4096]{1,0:T(8,128)} fusion(bf16[512,2,4096]{2,0,1:T(8,128)(2,1)} %all-gather.2.cloned.1.call-done, f32[2,1024,512]{1,0,2:T(2,128)} %select_bitcast_fusion), kind=kOutput, calls=%fused_computation.1 | convolution fusion | flops 51539607552 | bytes 29360128 | tf_op jit(solution)/shard_map/crk,kcn->rn/dot_general | solution.py:33
  (14 shorter events, 0.3 us)
Async XLA Ops:
  6.5 5.1 %copy-start.1 = (s32[4]{0:T(128)S(1)}, s32[4]{0:T(128)}, u32[]{:S(2)}) copy-start(s32[4]{0:T(128)} %param.6) | copy-start | bytes 52
  6.5 35.5 %copy-start = (s32[9]{0:T(128)S(1)}, s32[9]{0:T(128)}, u32[]{:S(2)}) copy-start(s32[9]{0:T(128)} %param.7) | copy-start | bytes 112
  6.5 130.2 %all-gather.2.cloned.1.call-start = ((), (), s32[]{:S(2)}) async-start(), calls=%async_computation | async-start | bytes 9437184 | tf_op jit(solution)/shard_map/all_gather | solution.py:36
  12.8 14.9 %collective-permute-start = (f32[2,1024,128]{1,0,2:T(2,128)S(1)}, f32[2,1024,128]{1,0,2:T(2,128)S(1)}, u32[]{:S(2)}, u32[]{:S(2)}) collective-permute-start(f32[2,1024,128]{1,0,2:T(2,128)S(1)} %multiply_add_fusion), channel_id=1, source_target_pairs={{0,2},{2,4},{4,6},{6,0},{1,3},{3,5},{5,7},{7,1},{8,10},{10,12},{12... | collective-permute-start | bytes 3145736 | tf_op jit(solution)/shard_map/ppermute | solution.py:28
  27.7 14.3 %collective-permute-start.1 = (f32[2,1024,128]{1,0,2:T(2,128)S(1)}, f32[2,1024,128]{1,0,2:T(2,128)}, u32[]{:S(2)}, u32[]{:S(2)}) collective-permute-start(f32[2,1024,128]{1,0,2:T(2,128)S(1)} %collective-permute-done), channel_id=1, source_target_pairs={{0,2},{2,4},{4,6},{6,0},{1,3},{3,5},{5,7},{7,1},{8,10},{10,12},{12... | collective-permute-start | bytes 3145736 | tf_op jit(solution)/shard_map/ppermute | solution.py:28
  42.1 14.5 %collective-permute-start.2 = (f32[2,1024,128]{1,0,2:T(2,128)}, f32[2,1024,128]{1,0,2:T(2,128)}, u32[]{:S(2)}, u32[]{:S(2)}) collective-permute-start(f32[2,1024,128]{1,0,2:T(2,128)} %collective-permute-done.1), channel_id=1, source_target_pairs={{0,2},{2,4},{4,6},{6,0},{1,3},{3,5},{5,7},{7,1},{8,10},{10,12},{12... | collective-permute-start | bytes 3145736 | tf_op jit(solution)/shard_map/ppermute | solution.py:28
Sparse Core Ops, SparseCore 0:
  9.6 127.1 all-gather.1
